TPU v7x, 256 devices: a whole 4x4x8 slice. The times are simulated.
256 devices in a mesh: ka: 32 (over y, z_hi, x), occ: 8 (over z_lo, core).
Axes of the slice: x: 4, y: 4, z: 8 (z_hi: 2, z_lo: 4; z = z_hi * 4 + z_lo), core: 2. Of those that a mesh axis runs over, the one named last changes fastest.
Arguments:
- factors: bfloat16 [64, 8, 192, 2, 768], P('ka'), may hold values from -0.23925781 to 0.23925781
- occupied_energy: float32 [8], replicated, may hold values from -2 to -0.5
- virtual_energy: bfloat16 [64, 192], P('ka'), may hold values from 0.5 to 3
- conserve: int32 [64, 2], P('ka'), may hold values from 0 to 63, as said below
- pair_lists: int32 [2, 16, 2], P(None, 'occ'), may hold values from 0 to 7, as said below
Outputs:
- density: float32 [64, 192, 2, 192], P('ka', 'occ')
Inputs may be any that keep to these rules, and one draw needn't show every extreme that they name: For a momentum ka among the 2 momenta of block d (momenta d * 2 to d * 2 + 1), (64 - conserve[ka, r]) mod 64 lies in block (d - r - 1) mod 32; the 2 momenta of one block name different momenta in each round. `pair_lists`: each entry is an ordered pair (i, j) of occupied orbitals; every round begins with the pairs (0, 0) and (7, 7); within a round no ordered pair repeats (16 of the 64 ordered pairs appear).
All inputs are finite; a program needn't handle non-finite values.
Results may differ from a plain program's by a relative error of at most 0.00082.
Values may be sent and summed in bfloat16 or wider, within the bound.
No kernel may reach another device: no remote copies, remote signals or barrier semaphores. Data moves between devices by JAX's collectives and lax.ppermute only.
A program may use at most 128 MiB of HBM per device.

v0:
```python
import jax
import jax.numpy as jnp
from jax import lax
from jax.sharding import PartitionSpec as P


def from_behind(array, axis, by):
    size = lax.axis_size(axis)
    return lax.ppermute(array, axis, [(i, (i + by) % size) for i in range(size)])


def cut_along(array, dim, size):
    before, after = (array.shape[:dim], array.shape[dim + 1 :])
    return jnp.moveaxis(array.reshape(*before, size, -1, *after), dim, 0)


def sent_and_summed(array, axis, dim):
    size = lax.axis_size(axis)
    parts = lax.all_to_all(cut_along(array, dim, size), axis, 0, 0, tiled=True)
    return jnp.sum(parts, axis=0)


def build_mates(received, auxiliary):
    real_part = received[..., :auxiliary]
    imaginary = received[..., auxiliary:]
    turned = jnp.concatenate([-imaginary, real_part], axis=-1)
    return jnp.concatenate([received, turned], axis=-2)


def amplitude(left_rows, mate_rows, energy_left, energy_right, occupied_sum):
    values = lax.dot_general(
        left_rows, mate_rows, (((1,), (1,)), ((), ())), preferred_element_type=jnp.float32
    )
    denominator = energy_left[:, None] + energy_right[None, :] - occupied_sum
    return values / jnp.concatenate([denominator, denominator], axis=1)


def density_term(amplitudes, swapped):
    virtuals = amplitudes.shape[0]
    combined = (2.0 * amplitudes - swapped).astype(jnp.bfloat16)
    rounded = amplitudes.astype(jnp.bfloat16)
    turned = jnp.concatenate([-rounded[:, virtuals:], rounded[:, :virtuals]], axis=1)
    stacked = jnp.concatenate([rounded, turned], axis=0)
    return lax.dot_general(
        combined, stacked, (((1,), (1,)), ((), ())), preferred_element_type=jnp.float32
    )


def pair_term(own_block, mate_block, energy_left, energy_right, occupied_energy, pair_row):
    leading = pair_row[0]
    trailing = pair_row[1]
    occupied_sum = occupied_energy[leading] + occupied_energy[trailing]
    amplitudes = amplitude(
        own_block[leading], mate_block[trailing], energy_left, energy_right, occupied_sum
    )
    swapped = amplitude(
        own_block[trailing], mate_block[leading], energy_left, energy_right, occupied_sum
    )
    return density_term(amplitudes, swapped)


def local(factors, occupied_energy, virtual_energy, conserve, pair_lists):
    momenta = factors.shape[0]
    orbitals = factors.shape[1]
    virtuals = factors.shape[2]
    auxiliary = factors.shape[4]
    own = factors.reshape(momenta, orbitals, virtuals, 2 * auxiliary)
    energy_own = virtual_energy.astype(jnp.float32)
    density = jnp.zeros((momenta, virtuals, 2 * virtuals), jnp.float32)
    for round_index in range(conserve.shape[1]):
        portion = orbitals // lax.axis_size("occ")
        portion_block = lax.dynamic_slice_in_dim(
            factors, lax.axis_index("occ") * portion, portion, 1
        )
        shifted, energy_mate = from_behind((portion_block, virtual_energy), "ka", round_index + 1)
        received = lax.all_gather(shifted, "occ", axis=1, tiled=True)
        mates = build_mates(received.reshape(momenta, orbitals, virtuals, 2 * auxiliary), auxiliary)
        energy_mate = energy_mate.astype(jnp.float32)
        for local_index in range(momenta):
            chosen = (momenta - conserve[local_index, round_index] % momenta) % momenta
            mate_block = lax.dynamic_index_in_dim(mates, chosen, 0, keepdims=False)
            energy_right = lax.dynamic_index_in_dim(energy_mate, chosen, 0, keepdims=False)
            own_block = own[local_index]
            energy_left = energy_own[local_index]

            def add_pair(partial_sum, pair_row):
                term = pair_term(
                    own_block, mate_block, energy_left, energy_right, occupied_energy, pair_row
                )
                return (partial_sum + term, None)

            running, ignored = lax.scan(add_pair, density[local_index], pair_lists[round_index])
            density = density.at[local_index].set(running)
    shaped = density.reshape(momenta, virtuals, 2, virtuals)
    return sent_and_summed(shaped, "occ", 1)


def solution(mesh):
    in_specs = (
        P("ka", None, None, None, None),
        P(),
        P("ka", None),
        P("ka", None),
        P(None, "occ", None),
    )
    out_specs = P("ka", "occ", None, None)
    return jax.shard_map(local, mesh=mesh, in_specs=in_specs, out_specs=out_specs, check_vma=False)
```

profile of v0, /device:TPU:1, one launch (start us, length us, event | category | flops | bytes accessed | tf_op | source)
XLA Modules:
  0.0 440.6 jit_solution(3128078142213431730)
XLA Ops:
  6.5 2.1 constant_dynamic-slice_fusion.8
  8.6 2.1 collective-permute-start
  10.7 43.4 %collective-permute-done = bf16[2,1,192,2,768]{4,3,2,1,0:T(2,128)(2,1)S(1)} collective-permute-done((bf16[2,1,192,2,768]{4,3,2,1,0:T(2,128)(2,1)S(1)}, bf16[2,1,192,2,768]{4,3,2,1,0:T(2,128)(2,1)S(1)}, u32[]{:S(2)}, u32[]{:S(2)}) %collective-permute-start) | collective-permute-done | bytes 1179680 | tf_op jit(solution)/shard_map/ppermute | solution.py:9
  54.2 1.0 copy-done.3
  55.4 33.9 %collective-permute-done.2 = bf16[2,1,192,2,768]{4,3,2,1,0:T(2,128)(2,1)S(1)} collective-permute-done((bf16[2,1,192,2,768]{4,3,2,1,0:T(2,128)(2,1)S(1)}, bf16[2,1,192,2,768]{4,3,2,1,0:T(2,128)(2,1)S(1)}, u32[]{:S(2)}, u32[]{:S(2)}) %collective-permute-start.2) | collective-permute-done | bytes 1179680 | tf_op jit(solution)/shard_map/ppermute | solution.py:9
  89.2 1.0 copy-done.2
  90.4 11.3 %collective-permute-start.3 = (bf16[2,192]{1,0:T(2,128)(2,1)}, bf16[2,192]{1,0:T(2,128)(2,1)S(1)}, u32[]{:S(2)}, u32[]{:S(2)}) collective-permute-start(bf16[2,192]{1,0:T(2,128)(2,1)} %param.23), channel_id=1, source_target_pairs={{0,16},{8,24},{16,32},{24,40},{32,48},{40,56},{48,64},{56,72},{64,... | collective-permute-start | bytes 2312 | tf_op jit(solution)/shard_map/ppermute | solution.py:9
  101.6 1.5 fusion.169
  111.1 0.8 fusion.170
  111.9 0.7 slice_bitcast_fusion.1
  112.6 9.8 %fusion.168 = (bf16[1,8,192,2,768]{4,3,2,1,0:T(2,128)(2,1)}, bf16[1,8,192,2,768]{4,3,2,1,0:T(2,128)(2,1)}) fusion(bf16[2,8,192,2,768]{4,3,2,1,0:T(2,128)(2,1)} %param.21), kind=kLoop, calls=%fused_computation.155 | loop fusion | bytes 18874368 | tf_op jit(solution)/shard_map/slice | solution.py:83
  122.4 11.3 %squeeze.153 = bf16[8,192,1536]{2,1,0:T(8,128)(2,1)} reshape(bf16[1,8,192,2,768]{4,3,2,1,0:T(2,128)(2,1)} %get-tuple-element.382) | data formatting | bytes 9437184 | tf_op jit(solution)/shard_map/squeeze | solution.py:83
  133.7 11.3 %squeeze.149 = bf16[8,192,1536]{2,1,0:T(8,128)(2,1)} reshape(bf16[1,8,192,2,768]{4,3,2,1,0:T(2,128)(2,1)} %get-tuple-element.381) | data formatting | bytes 9437184 | tf_op jit(solution)/shard_map/squeeze | solution.py:83
  145.0 50.5 %all-gather.3.cloned.1.call-done = bf16[2,8,192,2,768]{4,3,2,1,0:T(2,128)(2,1)} async-done(((bf16[2,1,192,2,768]{4,3,2,1,0:T(2,128)(2,1)}), bf16[2,8,192,2,768]{4,3,2,1,0:T(2,128)(2,1)}) %all-gather.3.cloned.1.call-update) | async-done | bytes 9437200 | tf_op jit(solution)/shard_map/all_gather | solution.py:76
  195.5 20.9 %reshape.159 = bf16[2,8,192,1536]{3,2,1,0:T(8,128)(2,1)} reshape(bf16[2,8,192,2,768]{4,3,2,1,0:T(2,128)(2,1)} %all-gather.3.cloned.1.call-done) | data formatting | bytes 18874368 | tf_op jit(solution)/shard_map/reshape | solution.py:77
  216.3 8.6 %slice_negate_fusion.5 = (bf16[2,8,192,768]{3,2,1,0:T(8,128)(2,1)}, bf16[2,8,192,768]{3,2,1,0:T(8,128)(2,1)}) fusion(bf16[2,8,192,1536]{3,2,1,0:T(8,128)(2,1)} %reshape.159), kind=kLoop, calls=%fused_computation.131 | loop fusion | flops 2359296 | bytes 18874368 | tf_op jit(solution)/shard_map/neg | solution.py:26
  225.0 6.3 %maximum_maximum_fusion = bf16[2,8,384,1536]{3,2,1,0:T(8,128)(2,1)S(1)} fusion(bf16[2,8,192,768]{3,2,1,0:T(8,128)(2,1)} %get-tuple-element.384, bf16[2,8,192,768]{3,2,1,0:T(8,128)(2,1)} %get-tuple-element.383, bf16[2,8,192,1536]{3,2,1,0:T(8,128)(2,1)S(1)} %copy-done), kind=kLoop, calls=%fused_computation.124 | loop fusion | flops 56623104 | bytes 37748736 | tf_op jit(solution)/shard_map/concatenate | solution.py:27
  231.4 6.9 %dynamic-slice_bitcast_fusion.3 = (bf16[8,384,1536]{2,1,0:T(8,128)(2,1)}, bf16[8,384,1536]{2,1,0:T(8,128)(2,1)}) fusion(bf16[2,8,384,1536]{3,2,1,0:T(8,128)(2,1)S(1)} %maximum_maximum_fusion, s32[]{:T(128)S(6)} %select_n.100, s32[]{:T(128)S(6)} %select_n.103), kind=kLoop, calls=%fused_computation.129 | loop fusion | bytes 37748744 | tf_op jit(solution)/shard_map/jit(dynamic_index_in_dim)/squeeze | solution.py:81
  238.3 21.6 %while.48 = (s32[]{:T(128)}, f32[192,384]{1,0:T(8,128)S(1)}, s32[2,2]{1,0:T(2,128)S(1)}, bf16[8,192,1536]{2,1,0:T(8,128)(2,1)}, bf16[8,384,1536]{2,1,0:T(8,128)(...) while((s32[]{:T(128)}, f32[192,384]{1,0:T(8,128)S(1)}, ...), condition=%wide.region_1.2_spmd.clone, body=%wide.region_0.1_spmd.clone.sunk | while | flops 511340544 | bytes 5900063 | solution.py:92
  238.3 0.6 fusion.210
  242.6 0.7 fusion.211
  244.5 2.0 fusion.212
  246.7 2.4 convolution_add_fusion.10
  249.1 0.6 fusion.210
  253.4 0.7 fusion.211
  255.3 2.0 fusion.212
  257.5 2.3 convolution_add_fusion.10
  259.8 0.7 copy-done.4
  260.5 1.0 copy.20
  261.5 21.6 %while.49 = (s32[]{:T(128)}, f32[192,384]{1,0:T(8,128)S(1)}, s32[2,2]{1,0:T(2,128)S(1)}, bf16[8,192,1536]{2,1,0:T(8,128)(2,1)}, bf16[8,384,1536]{2,1,0:T(8,128)(...) while((s32[]{:T(128)}, f32[192,384]{1,0:T(8,128)S(1)}, ...), condition=%wide.region_3.4_spmd.clone, body=%wide.region_2.3_spmd.clone.sunk | while | flops 511340544 | bytes 5900063 | solution.py:92
  261.5 0.6 fusion.216
  265.8 0.7 fusion.217
  267.8 2.0 fusion.218
  269.9 2.3 convolution_add_fusion.11
  272.3 0.6 fusion.216
  276.6 0.7 fusion.217
  278.6 2.0 fusion.218
  280.7 2.3 convolution_add_fusion.11
  283.1 36.5 %all-gather.5.cloned.1.call-done = bf16[2,8,192,2,768]{4,3,2,1,0:T(2,128)(2,1)} async-done(((bf16[2,1,192,2,768]{4,3,2,1,0:T(2,128)(2,1)}), bf16[2,8,192,2,768]{4,3,2,1,0:T(2,128)(2,1)}) %all-gather.5.cloned.1.call-update) | async-done | bytes 9437200 | tf_op jit(solution)/shard_map/all_gather | solution.py:76
  319.6 20.9 %reshape.161 = bf16[2,8,192,1536]{3,2,1,0:T(8,128)(2,1)} reshape(bf16[2,8,192,2,768]{4,3,2,1,0:T(2,128)(2,1)} %all-gather.5.cloned.1.call-done) | data formatting | bytes 18874368 | tf_op jit(solution)/shard_map/reshape | solution.py:77
  340.5 8.6 %slice_negate_fusion.4 = (bf16[2,8,192,768]{3,2,1,0:T(8,128)(2,1)}, bf16[2,8,192,768]{3,2,1,0:T(8,128)(2,1)}) fusion(bf16[2,8,192,1536]{3,2,1,0:T(8,128)(2,1)} %reshape.161), kind=kLoop, calls=%fused_computation.130 | loop fusion | flops 2359296 | bytes 18874368 | tf_op jit(solution)/shard_map/neg | solution.py:26
  349.1 6.3 %maximum_maximum_fusion.1 = bf16[2,8,384,1536]{3,2,1,0:T(8,128)(2,1)S(1)} fusion(bf16[2,8,192,768]{3,2,1,0:T(8,128)(2,1)} %get-tuple-element.380, bf16[2,8,192,768]{3,2,1,0:T(8,128)(2,1)} %get-tuple-element.379, bf16[2,8,192,1536]{3,2,1,0:T(8,128)(2,1)S(1)} %copy-done.1), kind=kLoop, calls=%fused_computation.125 | loop fusion | flops 56623104 | bytes 37748736 | tf_op jit(solution)/shard_map/concatenate | solution.py:27
  355.5 6.9 %dynamic-slice_bitcast_fusion = (bf16[8,384,1536]{2,1,0:T(8,128)(2,1)}, bf16[8,384,1536]{2,1,0:T(8,128)(2,1)}) fusion(bf16[2,8,384,1536]{3,2,1,0:T(8,128)(2,1)S(1)} %maximum_maximum_fusion.1, s32[]{:T(128)S(6)} %select_n.109, s32[]{:T(128)S(6)} %select_n.106), kind=kLoop, calls=%fused_computation.126 | loop fusion | bytes 37748744 | tf_op jit(solution)/shard_map/jit(dynamic_index_in_dim)/squeeze | solution.py:81
  362.4 21.7 %while.46 = (s32[]{:T(128)}, f32[192,384]{1,0:T(8,128)S(1)}, s32[2,2]{1,0:T(2,128)S(1)}, bf16[8,192,1536]{2,1,0:T(8,128)(2,1)}, bf16[8,384,1536]{2,1,0:T(8,128)(...) while((s32[]{:T(128)}, f32[192,384]{1,0:T(8,128)S(1)}, ...), condition=%wide.region_5.6_spmd, body=%wide.region_4.5_spmd.sunk | while | flops 511266816 | bytes 5900053 | solution.py:92
  362.4 0.6 fusion.198
  366.8 0.6 fusion.199
  368.8 2.0 fusion.200
  371.0 2.3 convolution_add_fusion.8
  373.3 0.6 fusion.198
  377.7 0.6 fusion.199
  379.7 2.0 fusion.200
  381.8 2.3 convolution_add_fusion.8
  384.2 22.2 %while.47 = (s32[]{:T(128)}, f32[192,384]{1,0:T(8,128)S(1)}, s32[2,2]{1,0:T(2,128)S(1)}, bf16[8,192,1536]{2,1,0:T(8,128)(2,1)}, bf16[8,384,1536]{2,1,0:T(8,128)(...) while((s32[]{:T(128)}, f32[192,384]{1,0:T(8,128)S(1)}, ...), condition=%wide.region_7.8_spmd, body=%wide.region_6.7_spmd.sunk | while | flops 511266816 | bytes 5900053 | solution.py:92
  384.3 0.6 fusion.204
  388.8 0.7 fusion.205
  390.9 2.0 fusion.206
  393.0 2.3 convolution_add_fusion.9
  395.4 0.6 fusion.204
  399.9 0.7 fusion.205
  402.0 2.0 fusion.206
  404.1 2.3 convolution_add_fusion.9
  406.4 0.6 reshape_reshape.3
  407.3 25.4 %all_to_all.5 = f32[8,2,24,2,192]{4,3,2,1,0:T(2,128)S(1)} all-to-all(f32[8,2,24,2,192]{4,3,2,1,0:T(2,128)S(1)} %copy.6), channel_id=1, replica_groups=mesh['ka'=32,'occ'=8] {'occ'}, dimensions={0} | all-to-all | bytes 1179648 | tf_op jit(solution)/shard_map/all_to_all | solution.py:19
  432.7 1.0 reduce_sum.9
  (60 shorter events, 2.4 us)
Async XLA Ops:
  6.5 188.9 %all-gather.3.cloned.1.call-start = ((), (), s32[]{:S(2)}) async-start(), calls=%async_computation.1 | async-start | bytes 10616832 | tf_op jit(solution)/shard_map/all_gather | solution.py:76
  8.6 45.5 %collective-permute-start = (bf16[2,1,192,2,768]{4,3,2,1,0:T(2,128)(2,1)S(1)}, bf16[2,1,192,2,768]{4,3,2,1,0:T(2,128)(2,1)S(1)}, u32[]{:S(2)}, u32[]{:S(2)}) collective-permute-start(bf16[2,1,192,2,768]{4,3,2,1,0:T(2,128)(2,1)S(1)} %constant_dynamic-slice_fusion.8), channel_id=1, source_target_pairs={{0,8},{8,16},{16,24},{24,32},{32,40},{40,48},{48,56},{56,64},{64,7... | collective-permute-start | bytes 3538952 | tf_op jit(solution)/shard_map/ppermute | solution.py:9
  54.2 1.0 copy-start.3
  55.2 264.4 %all-gather.5.cloned.1.call-start = ((), (), s32[]{:S(2)}) async-start(), calls=%async_computation.2 | async-start | bytes 10616832 | tf_op jit(solution)/shard_map/all_gather | solution.py:76
  55.3 34.0 %collective-permute-start.2 = (bf16[2,1,192,2,768]{4,3,2,1,0:T(2,128)(2,1)S(1)}, bf16[2,1,192,2,768]{4,3,2,1,0:T(2,128)(2,1)S(1)}, u32[]{:S(2)}, u32[]{:S(2)}) collective-permute-start(bf16[2,1,192,2,768]{4,3,2,1,0:T(2,128)(2,1)S(1)} %constant_dynamic-slice_fusion.8), channel_id=1, source_target_pairs={{0,16},{8,24},{16,32},{24,40},{32,48},{40,56},{48,64},{56,72},{64,... | collective-permute-start | bytes 3538952 | tf_op jit(solution)/shard_map/ppermute | solution.py:9
  89.2 1.0 copy-start.2
  90.3 54.7 %collective-permute-start.1 = (bf16[2,192]{1,0:T(2,128)(2,1)}, bf16[2,192]{1,0:T(2,128)(2,1)S(1)}, u32[]{:S(2)}, u32[]{:S(2)}) collective-permute-start(bf16[2,192]{1,0:T(2,128)(2,1)} %param.23), channel_id=1, source_target_pairs={{0,8},{8,16},{16,24},{24,32},{32,40},{40,48},{48,56},{56,64},{64,7... | collective-permute-start | bytes 2312 | tf_op jit(solution)/shard_map/ppermute | solution.py:9
  90.4 54.6 %collective-permute-start.3 = (bf16[2,192]{1,0:T(2,128)(2,1)}, bf16[2,192]{1,0:T(2,128)(2,1)S(1)}, u32[]{:S(2)}, u32[]{:S(2)}) collective-permute-start(bf16[2,192]{1,0:T(2,128)(2,1)} %param.23), channel_id=1, source_target_pairs={{0,16},{8,24},{16,32},{24,40},{32,48},{40,56},{48,64},{56,72},{64,... | collective-permute-start | bytes 2312 | tf_op jit(solution)/shard_map/ppermute | solution.py:9
  216.3 8.7 %copy-start = (bf16[2,8,192,1536]{3,2,1,0:T(8,128)(2,1)S(1)}, bf16[2,8,192,1536]{3,2,1,0:T(8,128)(2,1)}, u32[]{:S(2)}) copy-start(bf16[2,8,192,1536]{3,2,1,0:T(8,128)(2,1)} %reshape.159) | copy-start | bytes 28311556
  231.4 6.9 %copy-start.6 = (f32[8]{0:T(128)S(1)}, f32[8]{0:T(128)}, u32[]{:S(2)}) copy-start(f32[8]{0:T(128)} %param.22) | copy-start | bytes 100
  238.2 23.2 %copy-start.7 = (f32[192,384]{1,0:T(8,128)S(1)}, f32[192,384]{1,0:T(8,128)}, u32[]{:S(2)}) copy-start(f32[192,384]{1,0:T(8,128)} %custom-call.1) | copy-start | bytes 884740
  259.8 0.7 copy-start.4
  283.1 36.5 %copy-start.8 = (f32[192,384]{1,0:T(8,128)}, f32[192,384]{1,0:T(8,128)S(1)}, u32[]{:S(2)}) copy-start(f32[192,384]{1,0:T(8,128)S(1)} %get-tuple-element.222) | copy-start | bytes 884740
  340.5 8.7 %copy-start.1 = (bf16[2,8,192,1536]{3,2,1,0:T(8,128)(2,1)S(1)}, bf16[2,8,192,1536]{3,2,1,0:T(8,128)(2,1)}, u32[]{:S(2)}) copy-start(bf16[2,8,192,1536]{3,2,1,0:T(8,128)(2,1)} %reshape.161) | copy-start | bytes 28311556
  362.4 21.7 %copy-start.5 = (f32[192,384]{1,0:T(8,128)S(1)}, f32[192,384]{1,0:T(8,128)}, u32[]{:S(2)}) copy-start(f32[192,384]{1,0:T(8,128)} %copy-done.4) | copy-start | bytes 884740
  362.4 21.7 %copy-start.9 = (f32[192,384]{1,0:T(8,128)S(1)}, f32[192,384]{1,0:T(8,128)}, u32[]{:S(2)}) copy-start(f32[192,384]{1,0:T(8,128)} %copy-done.8) | copy-start | bytes 884740
Sparse Core Ops, SparseCore 0:
  55.3 140.0 all-gather.2
  197.3 122.2 all-gather.4
where the time goes:
time: 444 us; the launch traced here: 441 us
  waiting for transfers between devices  164 us (37%)
  local copies, waits for them, and re-layouts  108 us (24%)
  loops' own time  40.8 us (9%)
  matrix products  34.6 us (8%)
  other arithmetic  32.5 us (7%)
  blocking collectives  25.4 us (6%)
  between operations  21.6 us (5%)
  starting transfers between devices  13.6 us (3%)
    all_gather x2, waiting for transfers between devices, local(): received = lax.all_gather(shifted, 'occ', axis=1, tiled=True)  87 us
    ppermute x4, waiting for transfers between devices, from_behind(): lax.ppermute(array, axis, [(i, (i + by) % size) for i in range(size)])  77.3 us
    reshape x2, local copies, waits for them, and re-layouts, local(): received.reshape(momenta, orbitals, virtuals, 2 * auxiliary)  41.7 us
    another operation x4, loops' own time, local(): lax.scan(add_pair, density[local_index], pair_lists[round_index])  40.8 us
    all_to_all x1, blocking collectives, sent_and_summed(): parts = lax.all_to_all(cut_along(array, dim, size), axis, 0, 0, tiled=True)  25.4 us
    squeeze x2, local copies, waits for them, and re-layouts, local(): own_block = own[local_index]  22.6 us
    dot_general x8, matrix products, density_term(): lax.dot_general(combined, stacked, (((1,), (1,)), ((), ())), preferred_el...  18.4 us
    neg x2, other arithmetic, build_mates(): turned = jnp.concatenate([-imaginary, real_part], axis=-1)  17.2 us
  transfers between devices with their start and end apart: 6, of which 4 were waited for; matrix products, arithmetic and copies ran while one was open for 23% of the time, Pallas kernels for 0%

commit v1 on v0

--- a/solution.py
+++ b/solution.py
@@ -2,6 +2,11 @@
 import jax.numpy as jnp
 from jax import lax
 from jax.sharding import PartitionSpec as P
+
+
+def gather_over(x, axis, dim):
+    sent = jnp.stack([x] * lax.axis_size(axis))
+    return jnp.concatenate(lax.all_to_all(sent, axis, 0, 0), axis=dim)
 
 
 def from_behind(array, axis, by):
@@ -73,7 +78,7 @@
             factors, lax.axis_index("occ") * portion, portion, 1
         )
         shifted, energy_mate = from_behind((portion_block, virtual_energy), "ka", round_index + 1)
-        received = lax.all_gather(shifted, "occ", axis=1, tiled=True)
+        received = gather_over(shifted, "occ", 1)
         mates = build_mates(received.reshape(momenta, orbitals, virtuals, 2 * auxiliary), auxiliary)
         energy_mate = energy_mate.astype(jnp.float32)
         for local_index in range(momenta):

time: 444 us -> 702 us (1.58)
  waiting for transfers between devices: 164 us -> 359 us
  starting transfers between devices: 13.6 us -> 81.6 us
  between operations: 21.6 us -> 7.74 us
  local copies, waits for them, and re-layouts: 108 us -> 116 us
    ppermute x4, waiting for transfers between devices: 77.3 us -> 336 us  [from_behind(): lax.ppermute(array, axis, [(i, (i + by) % size) for i in range(size)])]
    all_gather x2 -> x0, waiting for transfers between devices: 87 us -> none  [local(): received = lax.all_gather(shifted, 'occ', axis=1, tiled=True)]
    another operation x0 -> x4, local copies, waits for them, and re-layouts: none -> 54.1 us  [the longest x2 41.8 us: local(): received.reshape(momenta, orbitals, virtuals, 2 * auxiliary)]
    reshape x2 -> x0, local copies, waits for them, and re-layouts: 41.7 us -> none  [local(): received.reshape(momenta, orbitals, virtuals, 2 * auxiliary)]
    ppermute x4, starting transfers between devices: 13.6 us -> 53 us  [from_behind(): lax.ppermute(array, axis, [(i, (i + by) % size) for i in range(size)])]
    all_to_all x0 -> x2, starting transfers between devices: none -> 28.5 us  [gather_over(): return jnp.concatenate(lax.all_to_all(sent, axis, 0, 0), axis=dim)]
    all_to_all x0 -> x2, waiting for transfers between devices: none -> 23.1 us  [gather_over(): return jnp.concatenate(lax.all_to_all(sent, axis, 0, 0), axis=dim)]
  transfers between devices with their start and end apart: 6 -> 6, of which waited for: 4 -> 4; matrix products, arithmetic and copies ran while one was open for 23% -> 14% of each run, Pallas kernels for 0% -> 0%
where the time goes in v1:
time: 702 us; the launch traced here: 698 us
  waiting for transfers between devices  359 us (51%)
  local copies, waits for them, and re-layouts  116 us (17%)
  starting transfers between devices  81.6 us (12%)
  loops' own time  40.9 us (6%)
  matrix products  34.5 us (5%)
  other arithmetic  32.4 us (5%)
  blocking collectives  25.5 us (4%)
  between operations  7.74 us (1%)
    ppermute x4, waiting for transfers between devices, from_behind(): lax.ppermute(array, axis, [(i, (i + by) % size) for i in range(size)])  336 us
    ppermute x4, starting transfers between devices, from_behind(): lax.ppermute(array, axis, [(i, (i + by) % size) for i in range(size)])  53 us
    another operation x2, local copies, waits for them, and re-layouts, local(): received.reshape(momenta, orbitals, virtuals, 2 * auxiliary)  41.8 us
    another operation x4, loops' own time, local(): lax.scan(add_pair, density[local_index], pair_lists[round_index])  40.9 us
    all_to_all x2, starting transfers between devices, gather_over(): return jnp.concatenate(lax.all_to_all(sent, axis, 0, 0), axis=dim)  28.5 us
    all_to_all x1, blocking collectives, sent_and_summed(): parts = lax.all_to_all(cut_along(array, dim, size), axis, 0, 0, tiled=True)  25.5 us
    all_to_all x2, waiting for transfers between devices, gather_over(): return jnp.concatenate(lax.all_to_all(sent, axis, 0, 0), axis=dim)  23.1 us
    squeeze x2, local copies, waits for them, and re-layouts, local(): own_block = own[local_index]  22.5 us
  transfers between devices with their start and end apart: 6, of which 4 were waited for; matrix products, arithmetic and copies ran while one was open for 14% of the time, Pallas kernels for 0%

profile of v1, /device:TPU:1, one launch (start us, length us, event | category | flops | bytes accessed | tf_op | source)
XLA Modules:
  0.0 698.2 jit_solution(11475505039707726185)
XLA Ops:
  0.0 2.1 constant_dynamic-slice_fusion.8
  2.1 2.1 collective-permute-start
  4.2 43.4 %collective-permute-done = bf16[2,1,192,2,768]{4,3,2,1,0:T(2,128)(2,1)S(1)} collective-permute-done((bf16[2,1,192,2,768]{4,3,2,1,0:T(2,128)(2,1)S(1)}, bf16[2,1,192,2,768]{4,3,2,1,0:T(2,128)(2,1)S(1)}, u32[]{:S(2)}, u32[]{:S(2)}) %collective-permute-start) | collective-permute-done | bytes 1179680 | tf_op jit(solution)/shard_map/ppermute | solution.py:14
  47.6 6.2 stack.4
  53.8 22.0 %all-to-all-start = ((bf16[8,2,1,192,2,768]{5,4,3,1,2,0:T(2,128)(2,1)}), bf16[8,2,1,192,2,768]{5,4,3,1,2,0:T(2,128)(2,1)}, u32[]{:S(2)}, u32[]{:S(2)}) async-start(bf16[8,2,1,192,2,768]{5,4,3,1,2,0:T(2,128)(2,1)} %stack.4), calls=%async_computation | async-start | bytes 18874368 | tf_op jit(solution)/shard_map/all_to_all | solution.py:9
  75.8 181.9 %collective-permute-done.2 = bf16[2,1,192,2,768]{4,3,2,1,0:T(2,128)(2,1)S(1)} collective-permute-done((bf16[2,1,192,2,768]{4,3,2,1,0:T(2,128)(2,1)S(1)}, bf16[2,1,192,2,768]{4,3,2,1,0:T(2,128)(2,1)S(1)}, u32[]{:S(2)}, u32[]{:S(2)}) %collective-permute-start.2) | collective-permute-done | bytes 1179680 | tf_op jit(solution)/shard_map/ppermute | solution.py:14
  257.8 23.1 %all-to-all-done = bf16[8,2,1,192,2,768]{5,4,3,1,2,0:T(2,128)(2,1)} async-done(((bf16[8,2,1,192,2,768]{5,4,3,1,2,0:T(2,128)(2,1)}), bf16[8,2,1,192,2,768]{5,4,3,1,2,0:T(2,128)(2,1)}, u32[]{:S(2)}, u32[]{:S(2)}) %all-to-all-start) | async-done | bytes 9437216 | tf_op jit(solution)/shard_map/all_to_all | solution.py:9
  280.9 6.2 stack.5
  287.1 6.5 all-to-all-start.1
  293.6 50.9 %collective-permute-start.3 = (bf16[2,192]{1,0:T(2,128)(2,1)S(1)}, bf16[2,192]{1,0:T(2,128)(2,1)S(1)}, u32[]{:S(2)}, u32[]{:S(2)}) collective-permute-start(bf16[2,192]{1,0:T(2,128)(2,1)S(1)} %copy-done.9), channel_id=1, source_target_pairs={{0,16},{8,24},{16,32},{24,40},{32,48},{40,56},{48,64},{56,72},{64,... | collective-permute-start | bytes 2312 | tf_op jit(solution)/shard_map/ppermute | solution.py:14
  344.5 0.6 fusion.169
  352.7 9.8 %fusion.168 = (bf16[1,8,192,2,768]{4,3,2,1,0:T(2,128)(2,1)}, bf16[1,8,192,2,768]{4,3,2,1,0:T(2,128)(2,1)}) fusion(bf16[2,8,192,2,768]{4,3,2,1,0:T(2,128)(2,1)} %param.21), kind=kLoop, calls=%fused_computation.155 | loop fusion | bytes 18874368 | tf_op jit(solution)/shard_map/slice | solution.py:88
  362.4 11.3 %squeeze.153 = bf16[8,192,1536]{2,1,0:T(8,128)(2,1)} reshape(bf16[1,8,192,2,768]{4,3,2,1,0:T(2,128)(2,1)} %get-tuple-element.382) | data formatting | bytes 9437184 | tf_op jit(solution)/shard_map/squeeze | solution.py:88
  373.7 11.3 %squeeze.149 = bf16[8,192,1536]{2,1,0:T(8,128)(2,1)} reshape(bf16[1,8,192,2,768]{4,3,2,1,0:T(2,128)(2,1)} %get-tuple-element.381) | data formatting | bytes 9437184 | tf_op jit(solution)/shard_map/squeeze | solution.py:88
  385.0 111.0 %collective-permute-done.1 = bf16[2,192]{1,0:T(2,128)(2,1)S(1)} collective-permute-done((bf16[2,192]{1,0:T(2,128)(2,1)S(1)}, bf16[2,192]{1,0:T(2,128)(2,1)S(1)}, u32[]{:S(2)}, u32[]{:S(2)}) %collective-permute-start.1) | collective-permute-done | bytes 800 | tf_op jit(solution)/shard_map/ppermute | solution.py:14
  496.0 20.9 %reshape_reshape.9 = bf16[2,8,192,1536]{3,2,0,1:T(8,128)(2,1)} reshape(bf16[2,8,1,192,2,768]{5,4,3,0,2,1:T(2,128)(2,1)} %bitcast.18) | data formatting | bytes 18874368 | tf_op jit(solution)/shard_map/reshape;reshape | solution.py:82
  516.9 8.6 %slice_negate_fusion.5 = (bf16[2,8,192,768]{3,2,0,1:T(8,128)(2,1)}, bf16[2,8,192,768]{3,2,0,1:T(8,128)(2,1)}) fusion(bf16[2,8,192,1536]{3,2,0,1:T(8,128)(2,1)} %reshape_reshape.9), kind=kLoop, calls=%fused_computation.131 | loop fusion | flops 2359296 | bytes 18874368 | tf_op jit(solution)/shard_map/neg | solution.py:31
  525.5 6.3 maximum_maximum_fusion
  531.8 6.9 dynamic-slice_bitcast_fusion.3
  538.7 21.8 %while.48 = (s32[]{:T(128)}, f32[192,384]{1,0:T(8,128)S(1)}, s32[2,2]{1,0:T(2,128)S(1)}, bf16[8,192,1536]{2,1,0:T(8,128)(2,1)}, bf16[8,384,1536]{2,1,0:T(8,128)(...) while((s32[]{:T(128)}, f32[192,384]{1,0:T(8,128)S(1)}, ...), condition=%wide.region_1.2_spmd.clone, body=%wide.region_0.1_spmd.clone.sunk | while | flops 511340544 | bytes 5900063 | solution.py:97
  538.7 0.7 fusion.210
  543.1 0.7 fusion.211
  545.2 2.0 fusion.212
  547.3 2.3 convolution_add_fusion.10
  549.6 0.7 fusion.210
  554.0 0.7 fusion.211
  556.1 2.0 fusion.212
  558.2 2.3 convolution_add_fusion.10
  560.5 0.7 copy-done.2
  561.3 1.0 copy.20
  562.2 21.8 %while.49 = (s32[]{:T(128)}, f32[192,384]{1,0:T(8,128)S(1)}, s32[2,2]{1,0:T(2,128)S(1)}, bf16[8,192,1536]{2,1,0:T(8,128)(2,1)}, bf16[8,384,1536]{2,1,0:T(8,128)(...) while((s32[]{:T(128)}, f32[192,384]{1,0:T(8,128)S(1)}, ...), condition=%wide.region_3.4_spmd.clone, body=%wide.region_2.3_spmd.clone.sunk | while | flops 511340544 | bytes 5900063 | solution.py:97
  562.2 0.6 fusion.216
  566.6 0.6 fusion.217
  568.7 2.0 fusion.218
  570.8 2.3 convolution_add_fusion.11
  573.1 0.6 fusion.216
  577.5 0.6 fusion.217
  579.5 2.0 fusion.218
  581.7 2.3 convolution_add_fusion.11
  584.0 0.7 copy-done.6
  584.7 20.9 %reshape_reshape.10 = bf16[2,8,192,1536]{3,2,0,1:T(8,128)(2,1)} reshape(bf16[2,8,1,192,2,768]{5,4,3,0,2,1:T(2,128)(2,1)} %bitcast.29) | data formatting | bytes 18874368 | tf_op jit(solution)/shard_map/reshape;reshape | solution.py:82
  605.6 8.6 %slice_negate_fusion.4 = (bf16[2,8,192,768]{3,2,0,1:T(8,128)(2,1)}, bf16[2,8,192,768]{3,2,0,1:T(8,128)(2,1)}) fusion(bf16[2,8,192,1536]{3,2,0,1:T(8,128)(2,1)} %reshape_reshape.10), kind=kLoop, calls=%fused_computation.130 | loop fusion | flops 2359296 | bytes 18874368 | tf_op jit(solution)/shard_map/neg | solution.py:31
  614.3 6.3 maximum_maximum_fusion.1
  620.6 6.7 dynamic-slice_bitcast_fusion
  627.3 21.7 %while.46 = (s32[]{:T(128)}, f32[192,384]{1,0:T(8,128)S(1)}, s32[2,2]{1,0:T(2,128)S(1)}, bf16[8,192,1536]{2,1,0:T(8,128)(2,1)}, bf16[8,384,1536]{2,1,0:T(8,128)(...) while((s32[]{:T(128)}, f32[192,384]{1,0:T(8,128)S(1)}, ...), condition=%wide.region_5.6_spmd, body=%wide.region_4.5_spmd.sunk | while | flops 511266816 | bytes 5900053 | solution.py:97
  627.3 0.6 fusion.198
  631.8 0.6 fusion.199
  633.8 2.0 fusion.200
  635.9 2.3 convolution_add_fusion.8
  638.2 0.6 fusion.198
  642.6 0.6 fusion.199
  644.6 2.0 fusion.200
  646.8 2.3 convolution_add_fusion.8
  649.2 21.6 %while.47 = (s32[]{:T(128)}, f32[192,384]{1,0:T(8,128)S(1)}, s32[2,2]{1,0:T(2,128)S(1)}, bf16[8,192,1536]{2,1,0:T(8,128)(2,1)}, bf16[8,384,1536]{2,1,0:T(8,128)(...) while((s32[]{:T(128)}, f32[192,384]{1,0:T(8,128)S(1)}, ...), condition=%wide.region_7.8_spmd, body=%wide.region_6.7_spmd.sunk | while | flops 511266816 | bytes 5900053 | solution.py:97
  649.2 0.6 fusion.204
  653.6 0.6 fusion.205
  655.6 2.0 fusion.206
  657.7 2.3 convolution_add_fusion.9
  660.0 0.6 fusion.204
  664.4 0.6 fusion.205
  666.4 2.0 fusion.206
  668.5 2.3 convolution_add_fusion.9
  671.7 25.5 %all_to_all.15 = f32[8,2,24,2,192]{4,3,2,1,0:T(2,128)S(1)} all-to-all(f32[8,2,24,2,192]{4,3,2,1,0:T(2,128)S(1)} %copy.6), channel_id=1, replica_groups=mesh['ka'=32,'occ'=8] {'occ'}, dimensions={0} | all-to-all | bytes 1179648 | tf_op jit(solution)/shard_map/all_to_all | solution.py:24
  697.2 1.0 reduce_sum.9
  (62 shorter events, 2.7 us)
Async XLA Ops:
  2.1 45.5 %collective-permute-start = (bf16[2,1,192,2,768]{4,3,2,1,0:T(2,128)(2,1)S(1)}, bf16[2,1,192,2,768]{4,3,2,1,0:T(2,128)(2,1)S(1)}, u32[]{:S(2)}, u32[]{:S(2)}) collective-permute-start(bf16[2,1,192,2,768]{4,3,2,1,0:T(2,128)(2,1)S(1)} %constant_dynamic-slice_fusion.8), channel_id=1, source_target_pairs={{0,8},{8,16},{16,24},{24,32},{32,40},{40,48},{48,56},{56,64},{64,7... | collective-permute-start | bytes 3538952 | tf_op jit(solution)/shard_map/ppermute | solution.py:14
  53.8 227.0 %all-to-all-start = ((bf16[8,2,1,192,2,768]{5,4,3,1,2,0:T(2,128)(2,1)}), bf16[8,2,1,192,2,768]{5,4,3,1,2,0:T(2,128)(2,1)}, u32[]{:S(2)}, u32[]{:S(2)}) async-start(bf16[8,2,1,192,2,768]{5,4,3,1,2,0:T(2,128)(2,1)} %stack.4), calls=%async_computation | async-start | bytes 18874368 | tf_op jit(solution)/shard_map/all_to_all | solution.py:9
  75.8 181.9 %collective-permute-start.2 = (bf16[2,1,192,2,768]{4,3,2,1,0:T(2,128)(2,1)S(1)}, bf16[2,1,192,2,768]{4,3,2,1,0:T(2,128)(2,1)S(1)}, u32[]{:S(2)}, u32[]{:S(2)}) collective-permute-start(bf16[2,1,192,2,768]{4,3,2,1,0:T(2,128)(2,1)S(1)} %constant_dynamic-slice_fusion.8), channel_id=1, source_target_pairs={{0,16},{8,24},{16,32},{24,40},{32,48},{40,56},{48,64},{56,72},{64,... | collective-permute-start | bytes 3538952 | tf_op jit(solution)/shard_map/ppermute | solution.py:14
  287.0 6.5 copy-start.9
  287.0 57.5 %copy-start.8 = (s32[2,2]{1,0:T(2,128)S(1)}, s32[2,2]{1,0:T(2,128)}, u32[]{:S(2)}) copy-start(s32[2,2]{1,0:T(2,128)} %param.24) | copy-start | bytes 52
  287.0 65.6 %copy-start.10 = (s32[2,2,2]{2,1,0:T(2,128)S(1)}, s32[2,2,2]{2,1,0:T(2,128)}, u32[]{:S(2)}) copy-start(s32[2,2,2]{2,1,0:T(2,128)} %param.25) | copy-start | bytes 100
  287.1 297.0 %all-to-all-start.1 = ((bf16[8,2,1,192,2,768]{5,4,3,1,2,0:T(2,128)(2,1)}), bf16[8,2,1,192,2,768]{5,4,3,1,2,0:T(2,128)(2,1)}, u32[]{:S(2)}, u32[]{:S(2)}) async-start(bf16[8,2,1,192,2,768]{5,4,3,1,2,0:T(2,128)(2,1)} %stack.5), calls=%async_computation.1 | async-start | bytes 18874368 | tf_op jit(solution)/shard_map/all_to_all | solution.py:9
  293.6 202.4 %collective-permute-start.1 = (bf16[2,192]{1,0:T(2,128)(2,1)S(1)}, bf16[2,192]{1,0:T(2,128)(2,1)S(1)}, u32[]{:S(2)}, u32[]{:S(2)}) collective-permute-start(bf16[2,192]{1,0:T(2,128)(2,1)S(1)} %copy-done.9), channel_id=1, source_target_pairs={{0,8},{8,16},{16,24},{24,32},{32,40},{40,48},{48,56},{56,64},{64,7... | collective-permute-start | bytes 2312 | tf_op jit(solution)/shard_map/ppermute | solution.py:14
  293.6 202.4 %collective-permute-start.3 = (bf16[2,192]{1,0:T(2,128)(2,1)S(1)}, bf16[2,192]{1,0:T(2,128)(2,1)S(1)}, u32[]{:S(2)}, u32[]{:S(2)}) collective-permute-start(bf16[2,192]{1,0:T(2,128)(2,1)S(1)} %copy-done.9), channel_id=1, source_target_pairs={{0,16},{8,24},{16,32},{24,40},{32,48},{40,56},{48,64},{56,72},{64,... | collective-permute-start | bytes 2312 | tf_op jit(solution)/shard_map/ppermute | solution.py:14
  516.9 8.7 %copy-start = (bf16[2,8,192,1536]{3,2,0,1:T(8,128)(2,1)S(1)}, bf16[2,8,192,1536]{3,2,0,1:T(8,128)(2,1)}, u32[]{:S(2)}) copy-start(bf16[2,8,192,1536]{3,2,0,1:T(8,128)(2,1)} %reshape_reshape.9) | copy-start | bytes 28311556
  531.8 6.9 copy-start.4
  538.7 23.5 %copy-start.5 = (f32[192,384]{1,0:T(8,128)S(1)}, f32[192,384]{1,0:T(8,128)}, u32[]{:S(2)}) copy-start(f32[192,384]{1,0:T(8,128)} %custom-call.1) | copy-start | bytes 884740
  560.5 0.7 copy-start.2
  584.0 0.7 copy-start.6
  605.6 8.7 %copy-start.1 = (bf16[2,8,192,1536]{3,2,0,1:T(8,128)(2,1)S(1)}, bf16[2,8,192,1536]{3,2,0,1:T(8,128)(2,1)}, u32[]{:S(2)}) copy-start(bf16[2,8,192,1536]{3,2,0,1:T(8,128)(2,1)} %reshape_reshape.10) | copy-start | bytes 28311556
  627.3 21.7 %copy-start.3 = (f32[192,384]{1,0:T(8,128)S(1)}, f32[192,384]{1,0:T(8,128)}, u32[]{:S(2)}) copy-start(f32[192,384]{1,0:T(8,128)} %copy-done.2) | copy-start | bytes 884740
  627.3 21.7 %copy-start.7 = (f32[192,384]{1,0:T(8,128)S(1)}, f32[192,384]{1,0:T(8,128)}, u32[]{:S(2)}) copy-start(f32[192,384]{1,0:T(8,128)} %copy-done.6) | copy-start | bytes 884740
